TPU v7x, 256 devices: a whole 4x4x8 slice. The times are simulated.
256 devices in a mesh: seq: 64 (over y, z, core), tab: 4 (over x).
Axes of the slice: x: 4, y: 4, z: 8, core: 2. Of those that a mesh axis runs over, the one named last changes fastest.
Arguments:
- cotangent: bfloat16 [65536, 2560], P('seq', 'tab'), may hold values from -6 to 6
- saved_value: bfloat16 [65536, 2560], P('seq', 'tab'), may hold values from -6 to 6
- gate_scale: float32 [65536], P('seq'), may hold values from 0.2 to 1
- conv_weight: float32 [4, 2560], P(None, 'tab'), may hold values from -3 to 3
- value_weight: bfloat16 [1280, 2560], P(None, 'tab'), may hold values from -0.25 to 0.25
- owner_ids: int32 [8, 65536, 1], P('tab', 'seq'), may hold values from 0 to 63; in each aligned block of 1024 rows (0 to 1023, 1024 to 2047, ..., all dimensions but the last counted through in order) at most 64 rows name the same one
- local_row: int32 [8, 65536], P('tab', 'seq'), may hold values from 0 to 511
- row_table: float32 [8, 32768, 160], P('tab', 'seq'), may hold values from -6 to 6
- moment_one: float32 [8, 32768, 160], P('tab', 'seq'), may hold values from -6 to 6
- moment_two: float32 [8, 32768, 160], P('tab', 'seq'), may hold values from 0.5 to 4
Outputs:
- new_table: float32 [8, 32768, 160], P('tab', 'seq')
- new_first: float32 [8, 32768, 160], P('tab', 'seq')
- new_second: float32 [8, 32768, 160], P('tab', 'seq')
Inputs may be any that keep to these rules, and one draw needn't show every extreme that they name: `owner_ids`: within each aligned block of 1024 tokens of one head (one device's tokens), no owner is named by more than 64 tokens; in some blocks one owner is named by exactly 64.
All inputs are finite; a program needn't handle non-finite values.
Results may differ from a plain program's by a relative error of at most 0.0029.
Values may be sent and summed in bfloat16 or wider, within the bound.
No kernel may reach another device: no remote copies, remote signals or barrier semaphores. Data moves between devices by JAX's collectives and lax.ppermute only.
A program may use at most 128 MiB of HBM per device.

v0:
```python
import jax
import jax.numpy as jnp
from jax import lax
from jax.sharding import PartitionSpec as P

beta_one = 0.9
beta_two = 0.95
learn_rate = 0.01
adam_steps = 10.0
epsilon = 1e-08


def from_behind(block, axis, distance):
    devices = range(lax.axis_size(axis))
    route = [(i - distance, i) for i in devices if i - distance in devices]
    return lax.ppermute(block, axis, route)


def causal_mix(context, conv_weight, length):
    mix_total = jnp.zeros((length, context.shape[1]), jnp.float32)
    for tap_index in range(4):
        row_start = 9 - 3 * tap_index
        mix_total = (
            mix_total + conv_weight[tap_index][None, :] * context[row_start : row_start + length]
        )
    return mix_total


def conv_adjoint(upstream, mixed_conv):
    squashed = jax.nn.sigmoid(mixed_conv)
    return upstream * squashed * (1.0 + mixed_conv * (1.0 - squashed))


def shards(
    cotangent,
    saved_value,
    gate_scale,
    conv_weight,
    value_weight,
    owner_ids,
    local_row,
    row_table,
    moment_one,
    moment_two,
):
    length = cotangent.shape[0]
    head_local = row_table.shape[0]
    table_rows = row_table.shape[1]
    head_dim = row_table.shape[2]
    own_width = head_local * head_dim
    peer_count = lax.axis_size("seq")
    count_cap = 4 * length // peer_count
    upstream = cotangent.astype(jnp.float32)
    value_rows = saved_value.astype(jnp.float32)
    prior_rows = from_behind(saved_value[length - 9 :], "seq", 1)
    context = jnp.concatenate([prior_rows.astype(jnp.float32), value_rows], axis=0)
    conv_grad = conv_adjoint(upstream, causal_mix(context, conv_weight, length))
    following = from_behind(conv_grad[:9], "seq", -1)
    extended = jnp.concatenate([conv_grad, following], axis=0)
    value_grad = upstream
    for tap_index in range(4):
        row_start = 3 * tap_index
        value_grad = (
            value_grad + conv_weight[tap_index][None, :] * extended[row_start : row_start + length]
        )
    scaled = (gate_scale[:, None] * value_grad).astype(jnp.bfloat16)
    full_term = lax.dot_general(
        value_weight, scaled, (((1,), (1,)), ((), ())), preferred_element_type=jnp.float32
    )
    summed = lax.psum(full_term, "tab")
    memory_grad = lax.dynamic_slice_in_dim(summed, lax.axis_index("tab") * own_width, own_width, 0)
    heads_grad = jnp.swapaxes(memory_grad.reshape(head_local, head_dim, length), 1, 2)
    owners = owner_ids[:, :, 0]
    position = jnp.arange(length, dtype=jnp.int32)
    earlier = position[None, :] < position[:, None]
    same_owner = owners[:, :, None] == owners[:, None, :]
    slot_rank = jnp.sum((same_owner & earlier[None]).astype(jnp.int32), axis=2)
    slot_index = owners * count_cap + slot_rank
    head_ids = jnp.broadcast_to(jnp.arange(head_local, dtype=jnp.int32)[:, None], slot_index.shape)
    send_grad = (
        jnp.zeros((head_local, peer_count * count_cap, head_dim), jnp.float32)
        .at[head_ids, slot_index]
        .set(heads_grad)
    )
    send_rows = (
        jnp.zeros((head_local, peer_count * count_cap), jnp.int32)
        .at[head_ids, slot_index]
        .set(local_row + 1)
    )
    send_grad = send_grad.reshape(head_local, peer_count, count_cap, head_dim)
    send_rows = send_rows.reshape(head_local, peer_count, count_cap)
    grads_in = lax.all_to_all(send_grad, "seq", split_axis=1, concat_axis=1, tiled=True)
    rows_in = lax.all_to_all(send_rows, "seq", split_axis=1, concat_axis=1, tiled=True)
    item_count = grads_in.shape[0]
    flat_rows = rows_in.reshape(item_count, -1) - 1
    flat_grads = grads_in.reshape(item_count, -1, head_dim)
    item_ids = jnp.broadcast_to(jnp.arange(item_count, dtype=jnp.int32)[:, None], flat_rows.shape)
    target = jnp.where(flat_rows < 0, table_rows, flat_rows)
    summed_rows = (
        jnp.zeros((item_count, table_rows, head_dim), jnp.float32)
        .at[item_ids, target]
        .add(flat_grads, mode="drop")
    )
    row_hits = (
        jnp.zeros((item_count, table_rows), jnp.int32).at[item_ids, target].add(1, mode="drop")
    )
    row_grad, row_hits = (summed_rows, row_hits)
    touched = (row_hits > 0)[:, :, None]
    first_next = beta_one * moment_one + (1.0 - beta_one) * row_grad
    second_next = beta_two * moment_two + (1.0 - beta_two) * row_grad * row_grad
    update = (
        first_next
        / (1.0 - beta_one**adam_steps)
        / (jnp.sqrt(second_next / (1.0 - beta_two**adam_steps)) + epsilon)
    )
    table_next = row_table - learn_rate * update
    return (
        jnp.where(touched, table_next, row_table),
        jnp.where(touched, first_next, moment_one),
        jnp.where(touched, second_next, moment_two),
    )


def solution(mesh):
    in_specs = (
        P("seq", "tab"),
        P("seq", "tab"),
        P("seq"),
        P(None, "tab"),
        P(None, "tab"),
        P("tab", "seq", None),
        P("tab", "seq"),
        P("tab", "seq", None),
        P("tab", "seq", None),
        P("tab", "seq", None),
    )
    out_specs = (P("tab", "seq", None), P("tab", "seq", None), P("tab", "seq", None))
    return jax.shard_map(shards, mesh=mesh, in_specs=in_specs, out_specs=out_specs, check_vma=False)
```

profile of v0, /device:TPU:1, one launch (start us, length us, event | category | flops | bytes accessed | tf_op | source)
XLA Modules:
  0.0 436.1 jit_solution(14999547283841224572)
XLA Ops:
  7.2 0.9 slice.42
  8.1 4.9 %collective-permute-start = (bf16[9,640]{1,0:T(8,128)(2,1)S(1)}, bf16[9,640]{1,0:T(8,128)(2,1)S(1)}, u32[]{:S(2)}, u32[]{:S(2)}) collective-permute-start(bf16[9,640]{1,0:T(8,128)(2,1)S(1)} %slice.42), channel_id=1, source_target_pairs={{0,4},{4,8},{8,12},{12,16},{16,20},{20,24},{24,28},{28,32},{32,36}... | collective-permute-start | bytes 34568 | tf_op jit(solution)/shard_map/ppermute | solution.py:16
  13.9 1.5 convert_element_type.17
  15.5 2.1 fusion.2
  17.6 1.9 collective-permute-start.1
  19.5 3.4 collective-permute-done.1
  22.9 6.8 %convolution_bitcast_fusion = f32[1280,1024]{0,1:T(8,128)} fusion(bf16[1280,640]{1,0:T(8,128)(2,1)S(1)} %copy-done, bf16[1024,640]{1,0:T(8,128)(2,1)S(1)} %copy-done.2, f32[9,640]{1,0:T(8,128)S(1)} %collective-permute-done.1, f32[1024,640]{1,0:T(8,128)S(1)} %fusion.2, f32[640]{0:T(1024)S(1)} %get-tuple-element.23, f32[640]{0:T(1024)S(1)} %get-tuple-element.24, ...), kind=kOutput, calls=%fused_computation.5 | convolution fusion | flops 1686896640 | bytes 10850816 | tf_op jit(solution)/shard_map/dot_general | solution.py:67
  30.7 1.9 convert_reduce_fusion
  32.9 8.1 %scatter_custom_fusion = s32[8192]{0:T(1024)S(1)} fusion(s32[2048]{0:T(1024)S(1)} %get-tuple-element.29, s32[2048]{0:T(1024)S(1)} %get-tuple-element.28, s32[]{:T(128)} %constant.19.clone.1), kind=kCustom, calls=%fused_computation.60 | custom fusion | bytes 32772
  41.8 11.6 %all-to-all-start = ((s32[64,1,128]{2,1,0:T(1,128)}), s32[64,1,128]{2,1,0:T(1,128)S(1)}, u32[]{:S(2)}, u32[]{:S(2)}) async-start(s32[64,1,128]{2,1,0:T(1,128)} %reshape.147), calls=%async_computation | async-start | bytes 65536 | tf_op jit(solution)/shard_map/all_to_all | solution.py:93
  53.5 93.5 %all-reduce.2.cloned.1.call-done = f32[1280,1024]{0,1:T(8,128)} async-done(((f32[1280,1024]{0,1:T(8,128)}), f32[1280,1024]{0,1:T(8,128)}) %all-reduce.2.cloned.1.call-update) | async-done | bytes 5242896 | tf_op jit(solution)/shard_map/psum | solution.py:70
  146.9 2.1 constant_dynamic-slice_fusion
  149.5 1.8 copy.116
  151.3 13.2 %scatter_custom_fusion.2 = f32[8192,160]{1,0:T(8,128)} fusion(s32[2048]{0:T(1024)S(1)} %get-tuple-element.29, f32[2048,160]{1,0:T(8,128)} %bitcast.36, f32[]{:T(128)} %constant.26.clone.1), kind=kCustom, calls=%fused_computation.6 | custom fusion | bytes 5243392
  164.5 7.7 %copy.104 = f32[2,64,64,160]{3,2,0,1:T(8,128)} copy(f32[2,64,64,160]{3,2,1,0:T(8,128)} %bitcast.32) | data formatting | bytes 10485760 | tf_op jit(solution)/shard_map/reshape | solution.py:90
  172.2 11.2 %all-to-all-start.1 = ((f32[2,64,64,160]{3,2,0,1:T(8,128)}), f32[2,64,64,160]{3,2,0,1:T(8,128)}, u32[]{:S(2)}, u32[]{:S(2)}) async-start(f32[2,64,64,160]{3,2,0,1:T(8,128)} %copy.104), calls=%async_computation.1 | async-start | bytes 16777216 | tf_op jit(solution)/shard_map/all_to_all | solution.py:92
  185.2 44.3 %scatter_custom_fusion.1 = s32[1024]{0:T(1024)S(1)} fusion(s32[8192]{0:T(1024)S(1)} %bitcast.40, s32[8192]{0:T(1024)S(1)} %broadcast.161, s32[]{:T(128)} %constant.19.clone.1), kind=kCustom, calls=%fused_computation.74 | custom fusion | flops 8192 | bytes 4100
  229.5 139.6 %all-to-all-done.1 = f32[2,64,64,160]{3,2,0,1:T(8,128)} async-done(((f32[2,64,64,160]{3,2,0,1:T(8,128)}), f32[2,64,64,160]{3,2,0,1:T(8,128)}, u32[]{:S(2)}, u32[]{:S(2)}) %all-to-all-start.1) | async-done | bytes 5242912 | tf_op jit(solution)/shard_map/all_to_all | solution.py:92
  369.1 7.7 %copy.119 = f32[2,64,64,160]{3,2,1,0:T(8,128)} copy(f32[2,64,64,160]{3,2,0,1:T(8,128)} %all-to-all-done.1) | data formatting | bytes 10485760 | tf_op jit(solution)/shard_map/reshape | solution.py:96
  376.8 44.9 %scatter_custom_fusion.3 = f32[1024,160]{1,0:T(8,128)S(1)} fusion(s32[8192]{0:T(1024)S(1)} %bitcast.41, f32[8192,160]{1,0:T(8,128)} %bitcast.33, f32[]{:T(128)} %constant.26.clone.1), kind=kCustom, calls=%fused_computation.48 | custom fusion | flops 1310720 | bytes 655872
  422.3 4.0 broadcast_select_fusion
  426.4 1.0 copy.113
  427.3 1.0 copy.114
  428.3 1.0 copy.115
  (57 shorter events, 5.8 us)
Async XLA Ops:
  7.2 15.8 %copy-start = (bf16[1280,640]{1,0:T(8,128)(2,1)S(1)}, bf16[1280,640]{1,0:T(8,128)(2,1)}, u32[]{:S(2)}) copy-start(bf16[1280,640]{1,0:T(8,128)(2,1)} %param.14) | copy-start | bytes 4915204
  7.2 8.3 %copy-start.2 = (bf16[1024,640]{1,0:T(8,128)(2,1)S(1)}, bf16[1024,640]{1,0:T(8,128)(2,1)}, u32[]{:S(2)}) copy-start(bf16[1024,640]{1,0:T(8,128)(2,1)} %param.10) | copy-start | bytes 3932164
  7.2 139.7 %all-reduce.2.cloned.1.call-start = ((), (), s32[]{:S(2)}) async-start(), calls=%async_computation.2 | async-start | bytes 10485760 | tf_op jit(solution)/shard_map/psum | solution.py:70
  8.1 7.3 %collective-permute-start = (bf16[9,640]{1,0:T(8,128)(2,1)S(1)}, bf16[9,640]{1,0:T(8,128)(2,1)S(1)}, u32[]{:S(2)}, u32[]{:S(2)}) collective-permute-start(bf16[9,640]{1,0:T(8,128)(2,1)S(1)} %slice.42), channel_id=1, source_target_pairs={{0,4},{4,8},{8,12},{12,16},{16,20},{20,24},{24,28},{28,32},{32,36}... | collective-permute-start | bytes 34568 | tf_op jit(solution)/shard_map/ppermute | solution.py:16
  15.5 7.5 %copy-start.10 = (f32[1024]{0:T(1024)S(1)}, f32[1024]{0:T(1024)}, u32[]{:S(2)}) copy-start(f32[1024]{0:T(1024)} %param.12) | copy-start | bytes 12292
  17.6 5.3 %collective-permute-start.1 = (f32[9,640]{1,0:T(8,128)S(1)}, f32[9,640]{1,0:T(8,128)S(1)}, u32[]{:S(2)}, u32[]{:S(2)}) collective-permute-start(f32[9,640]{1,0:T(8,128)S(1)} %slice.56), channel_id=1, source_target_pairs={{4,0},{8,4},{12,8},{16,12},{20,16},{24,20},{28,24},{32,28},{36,32}... | collective-permute-start | bytes 69128 | tf_op jit(solution)/shard_map/ppermute | solution.py:16
  29.7 0.7 copy-start.4
  29.7 2.9 copy-start.8
  29.7 3.0 copy-start.9
  29.7 3.1 copy-start.5
  41.8 130.3 %all-to-all-start = ((s32[64,1,128]{2,1,0:T(1,128)}), s32[64,1,128]{2,1,0:T(1,128)S(1)}, u32[]{:S(2)}, u32[]{:S(2)}) async-start(s32[64,1,128]{2,1,0:T(1,128)} %reshape.147), calls=%async_computation | async-start | bytes 65536 | tf_op jit(solution)/shard_map/all_to_all | solution.py:93
  172.2 12.7 %copy-start.7 = (s32[2]{0:T(128)S(1)}, s32[2]{0:T(128)}, u32[]{:S(2)}) copy-start(s32[2]{0:T(128)} %constant.63) | copy-start | bytes 28
  172.2 12.8 %copy-start.6 = (s32[2]{0:T(128)S(1)}, s32[2]{0:T(128)}, u32[]{:S(2)}) copy-start(s32[2]{0:T(128)} %constant.66) | copy-start | bytes 28
  172.2 196.9 %all-to-all-start.1 = ((f32[2,64,64,160]{3,2,0,1:T(8,128)}), f32[2,64,64,160]{3,2,0,1:T(8,128)}, u32[]{:S(2)}, u32[]{:S(2)}) async-start(f32[2,64,64,160]{3,2,0,1:T(8,128)} %copy.104), calls=%async_computation.1 | async-start | bytes 16777216 | tf_op jit(solution)/shard_map/all_to_all | solution.py:92
  376.8 45.5 %copy-start.3 = (f32[2,512,160]{1,2,0:T(8,128)S(1)}, f32[2,512,160]{1,2,0:T(8,128)}, u32[]{:S(2)}) copy-start(f32[2,512,160]{1,2,0:T(8,128)} %param.19) | copy-start | bytes 1966084
  422.3 6.9 %copy-start.1 = (bf16[1280,640]{1,0:T(8,128)(2,1)S(1)}, bf16[1280,640]{1,0:T(8,128)(2,1)}, u32[]{:S(2)}) copy-start(bf16[1280,640]{1,0:T(8,128)(2,1)} %param.14) | copy-start | bytes 4915204
Sparse Core Ops, SparseCore 0:
  29.9 117.0 all-reduce.1
where the time goes:
time: 437 us; the launch traced here: 436 us
  waiting for transfers between devices  236 us (54%)
  other arithmetic  100 us (23%)
  local copies, waits for them, and re-layouts  48.5 us (11%)
  starting transfers between devices  29.7 us (7%)
  between operations  14.4 us (3%)
  matrix products  6.78 us (2%)
    all_to_all x1, waiting for transfers between devices, shards(): lax.all_to_all(send_grad, 'seq', split_axis=1, concat_axis=1, tiled=True)  140 us
    psum x1, waiting for transfers between devices, shards(): summed = lax.psum(full_term, 'tab')  93.5 us
    unnamed x9, other arithmetic  89.7 us
    unnamed x32, local copies, waits for them, and re-layouts  25.7 us
    all_to_all x1, starting transfers between devices, shards(): lax.all_to_all(send_rows, 'seq', split_axis=1, concat_axis=1, tiled=True)  11.6 us
    all_to_all x1, starting transfers between devices, shards(): lax.all_to_all(send_grad, 'seq', split_axis=1, concat_axis=1, tiled=True)  11.2 us
  transfers between devices with their start and end apart: 5, of which 3 were waited for; matrix products, arithmetic and copies ran while one was open for 19% of the time, Pallas kernels for 0%

commit v1 on v0

--- a/solution.py
+++ b/solution.py
@@ -67,7 +67,7 @@
     full_term = lax.dot_general(
         value_weight, scaled, (((1,), (1,)), ((), ())), preferred_element_type=jnp.float32
     )
-    summed = lax.psum(full_term, "tab")
+    summed = jnp.sum(lax.all_gather(full_term, "tab"), axis=0)
     memory_grad = lax.dynamic_slice_in_dim(summed, lax.axis_index("tab") * own_width, own_width, 0)
     heads_grad = jnp.swapaxes(memory_grad.reshape(head_local, head_dim, length), 1, 2)
     owners = owner_ids[:, :, 0]

time: 437 us -> 571 us (1.31)
  waiting for transfers between devices: 236 us -> 313 us
  other arithmetic: 100 us -> 132 us
  local copies, waits for them, and re-layouts: 48.5 us -> 73.8 us
    all_gather x0 -> x1, waiting for transfers between devices: none -> 171 us  [shards(): summed = jnp.sum(lax.all_gather(full_term, 'tab'), axis=0)]
    psum x1 -> x0, waiting for transfers between devices: 93.5 us -> none  [shards(): summed = lax.psum(full_term, 'tab')]
    reduce_sum x0 -> x1, other arithmetic: none -> 31.1 us  [shards(): summed = jnp.sum(lax.all_gather(full_term, 'tab'), axis=0)]
    all_gather x0 -> x1, local copies, waits for them, and re-layouts: none -> 25.3 us  [shards(): summed = jnp.sum(lax.all_gather(full_term, 'tab'), axis=0)]
  transfers between devices with their start and end apart: 5 -> 5, of which waited for: 3 -> 3; matrix products, arithmetic and copies ran while one was open for 19% -> 25% of each run, Pallas kernels for 0% -> 0%
where the time goes in v1:
time: 571 us; the launch traced here: 570 us
  waiting for transfers between devices  313 us (55%)
  other arithmetic  132 us (23%)
  local copies, waits for them, and re-layouts  73.8 us (13%)
  starting transfers between devices  29.7 us (5%)
  between operations  14.4 us (3%)
  matrix products  6.76 us (1%)
    all_gather x1, waiting for transfers between devices, shards(): summed = jnp.sum(lax.all_gather(full_term, 'tab'), axis=0)  171 us
    all_to_all x1, waiting for transfers between devices, shards(): lax.all_to_all(send_grad, 'seq', split_axis=1, concat_axis=1, tiled=True)  139 us
    unnamed x9, other arithmetic  89.9 us
    reduce_sum x1, other arithmetic, shards(): summed = jnp.sum(lax.all_gather(full_term, 'tab'), axis=0)  31.1 us
    unnamed x32, local copies, waits for them, and re-layouts  25.7 us
    all_gather x1, local copies, waits for them, and re-layouts, shards(): summed = jnp.sum(lax.all_gather(full_term, 'tab'), axis=0)  25.3 us
    all_to_all x1, starting transfers between devices, shards(): lax.all_to_all(send_rows, 'seq', split_axis=1, concat_axis=1, tiled=True)  11.6 us
  transfers between devices with their start and end apart: 5, of which 3 were waited for; matrix products, arithmetic and copies ran while one was open for 25% of the time, Pallas kernels for 0%

profile of v1, /device:TPU:1, one launch (start us, length us, event | category | flops | bytes accessed | tf_op | source)
XLA Modules:
  0.0 569.5 jit_solution(7509010087166068284)
XLA Ops:
  8.1 4.9 collective-permute-start
  13.9 1.5 convert_element_type.17
  15.5 2.1 fusion.2
  17.6 1.9 collective-permute-start.1
  19.5 3.4 collective-permute-done.1
  22.9 6.8 %convolution_bitcast_fusion = f32[1280,1024]{0,1:T(8,128)} fusion(bf16[1280,640]{1,0:T(8,128)(2,1)S(1)} %copy-done, bf16[1024,640]{1,0:T(8,128)(2,1)S(1)} %copy-done.2, f32[9,640]{1,0:T(8,128)S(1)} %collective-permute-done.1, f32[1024,640]{1,0:T(8,128)S(1)} %fusion.2, f32[640]{0:T(1024)S(1)} %get-tuple-element.23, f32[640]{0:T(1024)S(1)} %get-tuple-element.24, ...), kind=kOutput, calls=%fused_computation.5 | convolution fusion | flops 1686896640 | bytes 10850816 | tf_op jit(solution)/shard_map/dot_general | solution.py:67
  30.7 1.9 convert_reduce_fusion
  32.9 8.1 %scatter_custom_fusion = s32[8192]{0:T(1024)S(1)} fusion(s32[2048]{0:T(1024)S(1)} %get-tuple-element.29, s32[2048]{0:T(1024)S(1)} %get-tuple-element.28, s32[]{:T(128)} %constant.19.clone.1), kind=kCustom, calls=%fused_computation.60 | custom fusion | bytes 32772
  41.8 11.6 %all-to-all-start = ((s32[64,1,128]{2,1,0:T(1,128)}), s32[64,1,128]{2,1,0:T(1,128)S(1)}, u32[]{:S(2)}, u32[]{:S(2)}) async-start(s32[64,1,128]{2,1,0:T(1,128)} %reshape.148), calls=%async_computation | async-start | bytes 65536 | tf_op jit(solution)/shard_map/all_to_all | solution.py:93
  53.5 170.6 %all-gather.3.cloned.1.call-done = f32[5120,1024]{0,1:T(8,128)} async-done(((f32[1280,1024]{0,1:T(8,128)}), f32[5120,1024]{0,1:T(8,128)}) %all-gather.3.cloned.1.call-update) | async-done | bytes 20971536 | tf_op jit(solution)/shard_map/all_gather | solution.py:70
  224.1 25.3 %reshape.134 = f32[4,1280,1024]{1,0,2:T(4,128)} reshape(f32[5120,1024]{0,1:T(8,128)} %all-gather.3.cloned.1.call-done) | data formatting | bytes 41943040 | tf_op jit(solution)/shard_map/all_gather | solution.py:70
  249.3 31.1 %reduce_sum.22 = f32[1280,1024]{0,1:T(8,128)} reduce(f32[4,1280,1024]{1,0,2:T(4,128)} %reshape.134, f32[]{:T(128)} %constant.26.clone.1), dimensions={0}, to_apply=%region_3.0 | reduce | flops 3932160 | bytes 26214404 | tf_op jit(solution)/shard_map/reduce_sum | solution.py:70
  280.4 2.1 constant_dynamic-slice_fusion
  282.9 1.8 copy.113
  284.8 13.2 %scatter_custom_fusion.2 = f32[8192,160]{1,0:T(8,128)} fusion(s32[2048]{0:T(1024)S(1)} %get-tuple-element.29, f32[2048,160]{1,0:T(8,128)} %bitcast.38, f32[]{:T(128)} %constant.26.clone.1), kind=kCustom, calls=%fused_computation.6 | custom fusion | bytes 5243392
  297.9 7.7 %copy.101 = f32[2,64,64,160]{3,2,0,1:T(8,128)} copy(f32[2,64,64,160]{3,2,1,0:T(8,128)} %bitcast.34) | data formatting | bytes 10485760 | tf_op jit(solution)/shard_map/reshape | solution.py:90
  305.6 11.2 %all-to-all-start.1 = ((f32[2,64,64,160]{3,2,0,1:T(8,128)}), f32[2,64,64,160]{3,2,0,1:T(8,128)}, u32[]{:S(2)}, u32[]{:S(2)}) async-start(f32[2,64,64,160]{3,2,0,1:T(8,128)} %copy.101), calls=%async_computation.1 | async-start | bytes 16777216 | tf_op jit(solution)/shard_map/all_to_all | solution.py:92
  318.7 44.5 %scatter_custom_fusion.1 = s32[1024]{0:T(1024)S(1)} fusion(s32[8192]{0:T(1024)S(1)} %bitcast.42, s32[8192]{0:T(1024)S(1)} %broadcast.161, s32[]{:T(128)} %constant.19.clone.1), kind=kCustom, calls=%fused_computation.74 | custom fusion | flops 8192 | bytes 4100
  363.2 139.3 %all-to-all-done.1 = f32[2,64,64,160]{3,2,0,1:T(8,128)} async-done(((f32[2,64,64,160]{3,2,0,1:T(8,128)}), f32[2,64,64,160]{3,2,0,1:T(8,128)}, u32[]{:S(2)}, u32[]{:S(2)}) %all-to-all-start.1) | async-done | bytes 5242912 | tf_op jit(solution)/shard_map/all_to_all | solution.py:92
  502.6 7.7 %copy.116 = f32[2,64,64,160]{3,2,1,0:T(8,128)} copy(f32[2,64,64,160]{3,2,0,1:T(8,128)} %all-to-all-done.1) | data formatting | bytes 10485760 | tf_op jit(solution)/shard_map/reshape | solution.py:96
  510.3 44.9 %scatter_custom_fusion.3 = f32[1024,160]{1,0:T(8,128)S(1)} fusion(s32[8192]{0:T(1024)S(1)} %bitcast.43, f32[8192,160]{1,0:T(8,128)} %bitcast.35, f32[]{:T(128)} %constant.26.clone.1), kind=kCustom, calls=%fused_computation.48 | custom fusion | flops 1310720 | bytes 655872
  555.8 4.0 broadcast_select_fusion
  559.8 1.0 copy.110
  560.8 1.0 copy.111
  (59 shorter events, 7.7 us)
Async XLA Ops:
  7.2 15.8 %copy-start = (bf16[1280,640]{1,0:T(8,128)(2,1)S(1)}, bf16[1280,640]{1,0:T(8,128)(2,1)}, u32[]{:S(2)}) copy-start(bf16[1280,640]{1,0:T(8,128)(2,1)} %param.14) | copy-start | bytes 4915204
  7.2 8.3 %copy-start.2 = (bf16[1024,640]{1,0:T(8,128)(2,1)S(1)}, bf16[1024,640]{1,0:T(8,128)(2,1)}, u32[]{:S(2)}) copy-start(bf16[1024,640]{1,0:T(8,128)(2,1)} %param.10) | copy-start | bytes 3932164
  7.2 216.9 %all-gather.3.cloned.1.call-start = ((), (), s32[]{:S(2)}) async-start(), calls=%async_computation.2 | async-start | bytes 26214400 | tf_op jit(solution)/shard_map/all_gather | solution.py:70
  8.1 7.3 %collective-permute-start = (bf16[9,640]{1,0:T(8,128)(2,1)S(1)}, bf16[9,640]{1,0:T(8,128)(2,1)S(1)}, u32[]{:S(2)}, u32[]{:S(2)}) collective-permute-start(bf16[9,640]{1,0:T(8,128)(2,1)S(1)} %slice.42), channel_id=1, source_target_pairs={{0,4},{4,8},{8,12},{12,16},{16,20},{20,24},{24,28},{28,32},{32,36}... | collective-permute-start | bytes 34568 | tf_op jit(solution)/shard_map/ppermute | solution.py:16
  15.5 7.5 %copy-start.10 = (f32[1024]{0:T(1024)S(1)}, f32[1024]{0:T(1024)}, u32[]{:S(2)}) copy-start(f32[1024]{0:T(1024)} %param.12) | copy-start | bytes 12292
  17.6 5.3 collective-permute-start.1
  29.7 0.7 copy-start.4
  29.7 2.9 copy-start.8
  29.7 3.0 copy-start.9
  29.7 3.1 copy-start.5
  41.8 263.8 %all-to-all-start = ((s32[64,1,128]{2,1,0:T(1,128)}), s32[64,1,128]{2,1,0:T(1,128)S(1)}, u32[]{:S(2)}, u32[]{:S(2)}) async-start(s32[64,1,128]{2,1,0:T(1,128)} %reshape.148), calls=%async_computation | async-start | bytes 65536 | tf_op jit(solution)/shard_map/all_to_all | solution.py:93
  305.6 12.7 %copy-start.7 = (s32[2]{0:T(128)S(1)}, s32[2]{0:T(128)}, u32[]{:S(2)}) copy-start(s32[2]{0:T(128)} %constant.64) | copy-start | bytes 28
  305.6 12.8 %copy-start.6 = (s32[2]{0:T(128)S(1)}, s32[2]{0:T(128)}, u32[]{:S(2)}) copy-start(s32[2]{0:T(128)} %constant.67) | copy-start | bytes 28
  305.6 196.9 %all-to-all-start.1 = ((f32[2,64,64,160]{3,2,0,1:T(8,128)}), f32[2,64,64,160]{3,2,0,1:T(8,128)}, u32[]{:S(2)}, u32[]{:S(2)}) async-start(f32[2,64,64,160]{3,2,0,1:T(8,128)} %copy.101), calls=%async_computation.1 | async-start | bytes 16777216 | tf_op jit(solution)/shard_map/all_to_all | solution.py:92
  510.3 45.5 %copy-start.3 = (f32[2,512,160]{1,2,0:T(8,128)S(1)}, f32[2,512,160]{1,2,0:T(8,128)}, u32[]{:S(2)}) copy-start(f32[2,512,160]{1,2,0:T(8,128)} %param.19) | copy-start | bytes 1966084
  555.8 6.9 %copy-start.1 = (bf16[1280,640]{1,0:T(8,128)(2,1)S(1)}, bf16[1280,640]{1,0:T(8,128)(2,1)}, u32[]{:S(2)}) copy-start(bf16[1280,640]{1,0:T(8,128)(2,1)} %param.14) | copy-start | bytes 4915204
Sparse Core Ops, SparseCore 0:
  29.8 194.1 all-gather.2
